TPU v7x, 128 devices: a whole 4x4x4 slice. The times are simulated.
128 devices in a mesh: row: 8 (over z, core), col: 16 (over y, x).
Axes of the slice: x: 4, y: 4, z: 4, core: 2. Of those that a mesh axis runs over, the one named last changes fastest.
Arguments:
- right_side: float32 [8, 65536], P(None, ('row', 'col')), may hold values from -30 to 30
- u_factors: bfloat16 [128, 128, 48, 512], P(('row', 'col')), may hold values from -0.078125 to 0.078125
- v_factors: bfloat16 [128, 128, 48, 512], P('row', 'col'), may hold values from -0.25 to 0.25
- ranks: int32 [128, 128], P('row', 'col'), may hold values from 8 to 48
- far_blocks: bfloat16 [16, 512, 65536], P('row', None, 'col'), may hold values from -0.09375 to 0.09375
- block_target: int32 [16, 16], replicated, may hold values from 0 to 127, as said below
- recv_order: int32 [128], replicated, may hold values from 0 to 127, as said below
Outputs:
- densities: float32 [8, 65536], P(None, 'col')
- residual: float32 [8, 65536], P(None, ('row', 'col'))
- far_field: float32 [128, 4096], P(('row', 'col'))
Inputs may be any that keep to these rules, and one draw needn't show every extreme that they name: `recv_order`: a permutation of the receiver patches. `block_target`: block (b, c) with b % 2 == 0 lies on device g = (b // 2) * 16 + c; its receiver patch is stored in output rows owned by device (g + 128 / 2) mod 128 if g is even and by device g - 1 if g is odd; the other blocks may name any receiver patch.
All inputs are finite; a program needn't handle non-finite values.
Results may differ from a plain program's by a relative error of at most 0.008.
Values may be sent and summed in bfloat16 or wider, within the bound.
No kernel may reach another device: no remote copies, remote signals or barrier semaphores. Data moves between devices by JAX's collectives and lax.ppermute only.
A program may use at most 128 MiB of HBM per device.

v0:
```python
import jax
import jax.numpy as jnp
from jax import lax
from jax.sharding import PartitionSpec as P

ITERS = 2


def per_device(right_side, u_factors, v_factors, ranks, far_blocks, block_target, recv_order):
    dens_count = right_side.shape[0]
    own_rows = u_factors.shape[0]
    all_cols = u_factors.shape[1]
    slot_count = u_factors.shape[2]
    patch_len = u_factors.shape[3]
    group_rows = v_factors.shape[0]
    own_cols = v_factors.shape[1]
    slot_index = lax.broadcasted_iota(jnp.int32, (group_rows, own_cols, slot_count, 1), 2)
    kept = (slot_index < ranks[:, :, None, None]).astype(jnp.float32)
    kept_half = kept.astype(jnp.bfloat16)
    residual = right_side
    densities = jnp.zeros((dens_count, own_cols * patch_len), jnp.float32)
    for iteration in range(ITERS):
        res_bf = residual.astype(jnp.bfloat16).reshape(dens_count, own_rows, patch_len)
        back_coef = jnp.einsum(
            "ijsp,dip->ijsd", u_factors, res_bf, preferred_element_type=jnp.float32
        )
        back_coef = back_coef.astype(jnp.bfloat16).reshape(
            own_rows, all_cols, slot_count * dens_count
        )
        arrived = lax.all_to_all(back_coef, "col", split_axis=1, concat_axis=0, tiled=True)
        arrived = arrived.reshape(group_rows, own_cols, slot_count, dens_count) * kept_half
        partial_grad = jnp.einsum(
            "ijsp,ijsd->djp", v_factors, arrived, preferred_element_type=jnp.float32
        )
        grad = lax.psum(partial_grad.reshape(dens_count, own_cols * patch_len), "row")
        grad_local = jnp.sum(grad * grad, axis=1)
        grad_sq = lax.psum(grad_local, "col")
        grad_bf = grad.astype(jnp.bfloat16).reshape(dens_count, own_cols, patch_len)
        coefficients = (
            jnp.einsum("ijsp,djp->ijsd", v_factors, grad_bf, preferred_element_type=jnp.float32)
            * kept
        )
        coefficients = coefficients.astype(jnp.bfloat16).reshape(
            group_rows, own_cols, slot_count * dens_count
        )
        landed = lax.all_to_all(coefficients, "col", split_axis=0, concat_axis=1, tiled=True)
        landed = landed.reshape(own_rows, all_cols, slot_count, dens_count)
        image = jnp.einsum("ijsp,ijsd->dip", u_factors, landed, preferred_element_type=jnp.float32)
        image = image.reshape(dens_count, own_rows * patch_len)
        image_local = jnp.sum(image * image, axis=1)
        image_sq = lax.psum(image_local, ("row", "col"))
        step_size = grad_sq / (image_sq + 1e-06)
        densities = densities + step_size[:, None] * grad
        residual = residual - step_size[:, None] * image
    block_count = far_blocks.shape[0]
    x_half = densities.astype(jnp.bfloat16)
    block_field = jnp.einsum("bpn,dn->bdp", far_blocks, x_half, preferred_element_type=jnp.float32)
    block_field = block_field.reshape(block_count, dens_count * patch_len)
    local_target = lax.dynamic_slice(
        block_target, (lax.axis_index("row") * block_count, lax.axis_index("col")), (block_count, 1)
    ).reshape(block_count)
    onehot = (local_target[:, None] == recv_order[None, :]).astype(jnp.float32)
    far_field = lax.psum_scatter(
        jnp.dot(
            onehot.T,
            block_field,
            preferred_element_type=jnp.float32,
            precision=lax.Precision.HIGHEST,
        ),
        ("row", "col"),
        scatter_dimension=0,
        tiled=True,
    )
    return (densities, residual, far_field)


def solution(mesh):
    return jax.shard_map(
        per_device,
        mesh=mesh,
        in_specs=(
            P(None, ("row", "col")),
            P(("row", "col"), None, None, None),
            P("row", "col", None, None),
            P("row", "col"),
            P("row", None, "col"),
            P(),
            P(),
        ),
        out_specs=(P(None, "col"), P(None, ("row", "col")), P(("row", "col"), None)),
        check_vma=False,
    )
```

profile of v0, /device:TPU:1, one launch (start us, length us, event | category | flops | bytes accessed | tf_op | source)
XLA Modules:
  0.0 595.4 jit_solution(9957855549774173676)
XLA Ops:
  7.2 5.9 convolution_convert_fusion
  13.1 0.2 copy.50
  13.3 0.2 copy.51
  13.5 0.5 broadcast.22
  14.0 1.2 reduce.6
  15.2 0.7 reshape.129
  15.9 7.6 %all-to-all-start = ((bf16[16,2,1536]{2,1,0:T(2,128)(2,1)}), bf16[16,2,1536]{2,1,0:T(2,128)(2,1)S(1)}, u32[]{:S(2)}, u32[]{:S(2)}) async-start(bf16[16,2,1536]{2,1,0:T(2,128)(2,1)} %reshape.129), calls=%async_computation | async-start | bytes 196608 | tf_op jit(solution)/shard_map/all_to_all | solution.py:30
  23.6 0.1 fusion.38
  23.7 6.6 %all-to-all-done = bf16[16,2,1536]{2,1,0:T(2,128)(2,1)S(1)} async-done(((bf16[16,2,1536]{2,1,0:T(2,128)(2,1)}), bf16[16,2,1536]{2,1,0:T(2,128)(2,1)S(1)}, u32[]{:S(2)}, u32[]{:S(2)}) %all-to-all-start) | async-done | bytes 98336 | tf_op jit(solution)/shard_map/all_to_all | solution.py:30
  30.2 0.1 reshape.130
  30.3 0.6 bitcast_reduce_fusion.1
  30.9 1.8 reshape.105
  32.6 4.8 fusion.8
  37.4 58.2 %all-reduce.5.cloned.1.call-done = f32[8,4096]{1,0:T(8,128)} async-done(((f32[8,4096]{1,0:T(8,128)}), f32[8,4096]{1,0:T(8,128)}) %all-reduce.5.cloned.1.call-update) | async-done | bytes 131088 | tf_op jit(solution)/shard_map/psum | solution.py:35
  95.6 1.1 multiply_reduce_fusion.1
  96.7 5.9 fusion.22
  102.6 0.5 copy.55
  103.1 0.9 copy.56
  104.1 6.5 %all-to-all-start.1 = ((bf16[16,8,384]{2,1,0:T(8,128)(2,1)}), bf16[16,8,384]{2,1,0:T(8,128)(2,1)S(1)}, u32[]{:S(2)}, u32[]{:S(2)}) async-start(bf16[16,8,384]{2,1,0:T(8,128)(2,1)} %copy.56), calls=%async_computation.1 | async-start | bytes 196608 | tf_op jit(solution)/shard_map/all_to_all | solution.py:46
  110.6 33.3 %psum.43 = f32[8]{0:T(128)S(1)} all-reduce(f32[8]{0:T(128)S(1)} %get-tuple-element.5), channel_id=1, replica_groups=mesh['row'=8,'col'=16] {'col'}, use_global_device_ids=true, to_apply=%region_2.0 | all-reduce | flops 8 | bytes 64 | tf_op jit(solution)/shard_map/psum | solution.py:37
  144.0 1.8 reshape.109
  145.8 3.8 multiply_reduce_fusion.3
  149.6 72.1 %psum.44 = f32[8]{0:T(128)S(1)} all-reduce(f32[8]{0:T(128)S(1)} %get-tuple-element.9), channel_id=1, replica_groups=mesh['row'=8,'col'=16] {'row','col'}, use_global_device_ids=true, to_apply=%region_4.0 | all-reduce | flops 8 | bytes 64 | tf_op jit(solution)/shard_map/psum | solution.py:51
  221.7 9.4 %fusion.31 = bf16[1,128,384]{1,2,0:T(8,128)(2,1)S(1)} fusion(bf16[128,48,512]{2,1,0:T(8,128)(2,1)} %bitcast.81, f32[8,512]{1,0:T(8,128)S(1)} %copy-done.4, f32[8,512]{1,0:T(8,128)S(1)} %get-tuple-element.10, f32[8]{0:T(128)S(1)} %add_divide_fusion.1), kind=kOutput, calls=%fused_computation.18 | convolution fusion | flops 50393088 | bytes 6422560 | tf_op jit(solution)/shard_map/ijsp,dip->ijsd/dot_general | solution.py:24
  231.1 0.2 copy.59
  231.3 1.2 reduce.7
  232.6 10.2 %all_to_all.16 = bf16[16,2,1536]{2,1,0:T(2,128)(2,1)S(1)} all-to-all(bf16[16,2,1536]{2,1,0:T(2,128)(2,1)S(1)} %reshape.131), channel_id=1, replica_groups=mesh['row'=8,'col'=16] {'col'}, dimensions={0} | all-to-all | bytes 196608 | tf_op jit(solution)/shard_map/all_to_all | solution.py:30
  242.8 0.1 reshape.132
  242.9 0.6 bitcast_reduce_fusion
  243.5 1.8 reshape.111
  245.2 4.8 fusion.6
  250.1 55.2 %all-reduce.7.cloned.1.call-done = f32[8,4096]{1,0:T(8,128)} async-done(((f32[8,4096]{1,0:T(8,128)}), f32[8,4096]{1,0:T(8,128)}) %all-reduce.7.cloned.1.call-update) | async-done | bytes 131088 | tf_op jit(solution)/shard_map/psum | solution.py:35
  305.3 1.1 fusion.51
  306.4 5.9 fusion.25
  312.3 0.5 copy.62
  312.8 0.9 copy.63
  313.7 6.5 %all-to-all-start.3 = ((bf16[16,8,384]{2,1,0:T(8,128)(2,1)}), bf16[16,8,384]{2,1,0:T(8,128)(2,1)S(1)}, u32[]{:S(2)}, u32[]{:S(2)}) async-start(bf16[16,8,384]{2,1,0:T(8,128)(2,1)} %copy.63), calls=%async_computation.3 | async-start | bytes 196608 | tf_op jit(solution)/shard_map/all_to_all | solution.py:46
  320.3 0.2 dynamic-slice_reduce_fusion
  320.5 33.2 %psum.46 = f32[8]{0:T(128)S(1)} all-reduce(f32[8]{0:T(128)S(1)} %get-tuple-element.4), channel_id=1, replica_groups=mesh['row'=8,'col'=16] {'col'}, use_global_device_ids=true, to_apply=%region_7.0 | all-reduce | flops 8 | bytes 64 | tf_op jit(solution)/shard_map/psum | solution.py:37
  353.8 1.8 reshape.115
  355.5 3.8 multiply_reduce_fusion.2
  359.4 72.0 %psum.47 = f32[8]{0:T(128)S(1)} all-reduce(f32[8]{0:T(128)S(1)} %get-tuple-element.11), channel_id=1, replica_groups=mesh['row'=8,'col'=16] {'row','col'}, use_global_device_ids=true, to_apply=%region_9.0 | all-reduce | flops 8 | bytes 64 | tf_op jit(solution)/shard_map/psum | solution.py:51
  431.4 0.1 multiply_add_fusion
  431.5 5.7 convolution_bitcast_fusion
  437.3 2.4 fusion.44
  439.7 0.7 multiply_subtract_fusion
  440.4 146.9 %all-reduce.9.cloned.1.call-done = f32[128,4096]{1,0:T(8,128)} async-done(((f32[128,4096]{1,0:T(8,128)}), f32[128,4096]{1,0:T(8,128)}) %all-reduce.9.cloned.1.call-update) | async-done | bytes 2097168
  587.3 1.5 constant_dynamic-slice_fusion
  (27 shorter events, 0.3 us)
Async XLA Ops:
  7.2 313.2 %copy-start = (s32[16,16]{1,0:T(8,128)S(1)}, s32[16,16]{1,0:T(8,128)}, u32[]{:S(2)}) copy-start(s32[16,16]{1,0:T(8,128)} %param.12) | copy-start | bytes 3076
  7.2 16.4 %copy-start.5 = (s32[16,8]{0,1:T(8,128)S(1)}, s32[16,8]{0,1:T(8,128)}, u32[]{:S(2)}) copy-start(s32[16,8]{0,1:T(8,128)} %param.10) | copy-start | bytes 1540
  15.9 14.3 %all-to-all-start = ((bf16[16,2,1536]{2,1,0:T(2,128)(2,1)}), bf16[16,2,1536]{2,1,0:T(2,128)(2,1)S(1)}, u32[]{:S(2)}, u32[]{:S(2)}) async-start(bf16[16,2,1536]{2,1,0:T(2,128)(2,1)} %reshape.129), calls=%async_computation | async-start | bytes 196608 | tf_op jit(solution)/shard_map/all_to_all | solution.py:30
  23.5 72.1 %all-reduce.5.cloned.1.call-start = ((), (), s32[]{:S(2)}) async-start(), calls=%async_computation.4 | async-start | bytes 262144 | tf_op jit(solution)/shard_map/psum | solution.py:35
  102.6 119.1 %copy-start.4 = (f32[8,512]{1,0:T(8,128)S(1)}, f32[8,512]{1,0:T(8,128)}, u32[]{:S(2)}) copy-start(f32[8,512]{1,0:T(8,128)} %param.7) | copy-start | bytes 49156
  104.1 39.9 %all-to-all-start.1 = ((bf16[16,8,384]{2,1,0:T(8,128)(2,1)}), bf16[16,8,384]{2,1,0:T(8,128)(2,1)S(1)}, u32[]{:S(2)}, u32[]{:S(2)}) async-start(bf16[16,8,384]{2,1,0:T(8,128)(2,1)} %copy.56), calls=%async_computation.1 | async-start | bytes 196608 | tf_op jit(solution)/shard_map/all_to_all | solution.py:46
  110.6 194.7 %all-reduce.7.cloned.1.call-start = ((), (), s32[]{:S(2)}) async-start(), calls=%async_computation.5 | async-start | bytes 262144 | tf_op jit(solution)/shard_map/psum | solution.py:35
  312.3 119.2 %copy-start.2 = (f32[8,4096]{1,0:T(8,128)S(1)}, f32[8,4096]{1,0:T(8,128)}, u32[]{:S(2)}) copy-start(f32[8,4096]{1,0:T(8,128)} %all-reduce.5.cloned.1.call-done) | copy-start | bytes 393220
  312.3 119.2 %copy-start.3 = (f32[8,4096]{1,0:T(8,128)S(1)}, f32[8,4096]{1,0:T(8,128)}, u32[]{:S(2)}) copy-start(f32[8,4096]{1,0:T(8,128)} %all-reduce.7.cloned.1.call-done) | copy-start | bytes 393220
  313.7 40.0 %all-to-all-start.3 = ((bf16[16,8,384]{2,1,0:T(8,128)(2,1)}), bf16[16,8,384]{2,1,0:T(8,128)(2,1)S(1)}, u32[]{:S(2)}, u32[]{:S(2)}) async-start(bf16[16,8,384]{2,1,0:T(8,128)(2,1)} %copy.63), calls=%async_computation.3 | async-start | bytes 196608 | tf_op jit(solution)/shard_map/all_to_all | solution.py:46
  320.3 267.1 %all-reduce.9.cloned.1.call-start = ((), (), s32[]{:S(2)}) async-start(), calls=%async_computation.6 | async-start | bytes 4194304
  359.4 77.9 %copy-start.6 = (s32[128]{0:T(128)S(1)}, s32[128]{0:T(128)}, u32[]{:S(2)}) copy-start(s32[128]{0:T(128)} %param.13) | copy-start | bytes 1540
  431.5 8.2 %copy-start.1 = (f32[8,4096]{1,0:T(8,128)}, f32[8,4096]{1,0:T(8,128)S(1)}, u32[]{:S(2)}) copy-start(f32[8,4096]{1,0:T(8,128)S(1)} %multiply_add_fusion) | copy-start | bytes 393220
Sparse Core Ops, SparseCore 0:
  37.6 58.0 all-reduce.4
  250.2 55.0 all-reduce.6
  439.8 147.4 all-reduce.8
where the time goes:
time: 596 us; the launch traced here: 595 us
  waiting for transfers between devices  267 us (45%)
  blocking collectives  221 us (37%)
  matrix products  52.3 us (9%)
  starting transfers between devices  20.8 us (3%)
  local copies, waits for them, and re-layouts  15 us (3%)
  between operations  14 us (2%)
    unnamed x4, waiting for transfers between devices  147 us
    psum x2, blocking collectives, per_device(): image_sq = lax.psum(image_local, ('row', 'col'))  144 us
    psum x2, waiting for transfers between devices, per_device(): lax.psum(partial_grad.reshape(dens_count, own_cols * patch_len), 'row')  113 us
    psum x2, blocking collectives, per_device(): grad_sq = lax.psum(grad_local, 'col')  66.6 us
    dot_general x2, matrix products, per_device(): jnp.einsum('ijsp,dip->ijsd', u_factors, res_bf, preferred_element_type=jn...  15.3 us
    all_to_all x2, starting transfers between devices, per_device(): lax.all_to_all(coefficients, 'col', split_axis=0, concat_axis=1, tiled=True)  13.1 us
  transfers between devices with their start and end apart: 6, of which 4 were waited for; matrix products, arithmetic and copies ran while one was open for 0% of the time, Pallas kernels for 0%

commit v1 on v0

--- a/solution.py
+++ b/solution.py
@@ -2,6 +2,7 @@
 import jax.numpy as jnp
 from jax import lax
 from jax.sharding import PartitionSpec as P
+from jax.lax import psum
 
 ITERS = 2
 
@@ -48,7 +49,9 @@
         image = jnp.einsum("ijsp,ijsd->dip", u_factors, landed, preferred_element_type=jnp.float32)
         image = image.reshape(dens_count, own_rows * patch_len)
         image_local = jnp.sum(image * image, axis=1)
-        image_sq = lax.psum(image_local, ("row", "col"))
+        image_sq = image_local
+        for jj in ("col", "row"):
+            image_sq = psum(image_sq, jj)
         step_size = grad_sq / (image_sq + 1e-06)
         densities = densities + step_size[:, None] * grad
         residual = residual - step_size[:, None] * image

time: 596 us -> 500 us (0.84)
  blocking collectives: 221 us -> 129 us
  starting transfers between devices: 20.8 us -> 14.2 us
    psum x2, blocking collectives: 144 us -> 46.7 us  [per_device(): image_sq = psum(image_sq, jj)]
    all_to_all x0 -> x1, blocking collectives: none -> 13 us  [per_device(): lax.all_to_all(coefficients, 'col', split_axis=0, concat_axis=1, tiled=True)]
    psum x2, blocking collectives: 66.6 us -> 59.9 us  [per_device(): grad_sq = lax.psum(grad_local, 'col')]
    all_to_all x2 -> x1, starting transfers between devices: 13.1 us -> 6.53 us  [per_device(): lax.all_to_all(coefficients, 'col', split_axis=0, concat_axis=1, tiled=True)]
    all_to_all x2 -> x1, waiting for transfers between devices: 0.01 us -> 6.41 us  [per_device(): lax.all_to_all(coefficients, 'col', split_axis=0, concat_axis=1, tiled=True)]
  transfers between devices with their start and end apart: 6 -> 5, of which waited for: 4 -> 5; matrix products, arithmetic and copies ran while one was open for 0% -> 0% of each run, Pallas kernels for 0% -> 0%
where the time goes in v1:
time: 500 us; the launch traced here: 499 us
  waiting for transfers between devices  270 us (54%)
  blocking collectives  129 us (26%)
  matrix products  52.3 us (10%)
  local copies, waits for them, and re-layouts  14.3 us (3%)
  starting transfers between devices  14.2 us (3%)
  between operations  14 us (3%)
  other arithmetic  5.57 us (1%)
    unnamed x4, waiting for transfers between devices  144 us
    psum x2, waiting for transfers between devices, per_device(): lax.psum(partial_grad.reshape(dens_count, own_cols * patch_len), 'row')  113 us
    psum x2, blocking collectives, per_device(): grad_sq = lax.psum(grad_local, 'col')  59.9 us
    psum x2, blocking collectives, per_device(): image_sq = psum(image_sq, jj)  46.7 us
    dot_general x2, matrix products, per_device(): jnp.einsum('ijsp,dip->ijsd', u_factors, res_bf, preferred_element_type=jn...  15.3 us
    all_to_all x1, blocking collectives, per_device(): lax.all_to_all(coefficients, 'col', split_axis=0, concat_axis=1, tiled=True)  13 us
    dot_general x2, matrix products, per_device(): jnp.einsum('ijsp,djp->ijsd', v_factors, grad_bf, preferred_element_type=j...  11.7 us
  transfers between devices with their start and end apart: 5, of which 5 were waited for; matrix products, arithmetic and copies ran while one was open for 0% of the time, Pallas kernels for 0%

profile of v1, /device:TPU:1, one launch (start us, length us, event | category | flops | bytes accessed | tf_op | source)
XLA Modules:
  0.0 498.8 jit_solution(5449829286960815218)
XLA Ops:
  7.2 5.9 %convolution_convert_fusion = bf16[128,48,8]{1,2,0:T(8,128)(2,1)S(1)} fusion(f32[8,512]{1,0:T(8,128)} %param.7, bf16[1,128,48,512]{3,2,1,0:T(8,128)(2,1)} %param.8), kind=kOutput, calls=%fused_computation.14 | convolution fusion | flops 50384896 | bytes 6406144 | tf_op jit(solution)/shard_map/ijsp,dip->ijsd/dot_general | solution.py:25
  13.1 0.2 copy.50
  13.3 0.2 copy.51
  13.5 0.5 broadcast.22
  14.0 1.2 reduce.6
  15.2 0.7 reshape.129
  15.9 7.6 %all-to-all-start = ((bf16[16,2,1536]{2,1,0:T(2,128)(2,1)}), bf16[16,2,1536]{2,1,0:T(2,128)(2,1)S(1)}, u32[]{:S(2)}, u32[]{:S(2)}) async-start(bf16[16,2,1536]{2,1,0:T(2,128)(2,1)} %reshape.129), calls=%async_computation | async-start | bytes 196608 | tf_op jit(solution)/shard_map/all_to_all | solution.py:31
  23.6 0.1 fusion.38
  23.7 6.6 %all-to-all-done = bf16[16,2,1536]{2,1,0:T(2,128)(2,1)S(1)} async-done(((bf16[16,2,1536]{2,1,0:T(2,128)(2,1)}), bf16[16,2,1536]{2,1,0:T(2,128)(2,1)S(1)}, u32[]{:S(2)}, u32[]{:S(2)}) %all-to-all-start) | async-done | bytes 98336 | tf_op jit(solution)/shard_map/all_to_all | solution.py:31
  30.2 0.1 reshape.130
  30.3 0.6 bitcast_reduce_fusion.1
  30.9 1.8 reshape.105
  32.6 4.8 fusion.8
  37.5 58.1 %all-reduce.7.cloned.1.call-done = f32[8,4096]{1,0:T(8,128)} async-done(((f32[8,4096]{1,0:T(8,128)}), f32[8,4096]{1,0:T(8,128)}) %all-reduce.7.cloned.1.call-update) | async-done | bytes 131088 | tf_op jit(solution)/shard_map/psum | solution.py:36
  95.6 1.1 multiply_reduce_fusion.1
  96.7 5.9 %fusion.22 = bf16[16,8,48,8]{2,3,0,1:T(8,128)(2,1)S(1)} fusion(bf16[8,8,512,1]{2,0,3,1:T(8,128)(2,1)S(1)} %bitcast.89, bf16[16,8,48,512]{3,2,1,0:T(8,128)(2,1)} %param.9, f32[16,8,48]{2,0,1:T(8,128)S(1)} %get-tuple-element.11), kind=kOutput, calls=%fused_computation.15 | convolution fusion | flops 50429952 | bytes 6479872 | tf_op jit(solution)/shard_map/ijsp,djp->ijsd/dot_general | solution.py:41
  102.6 0.5 copy.55
  103.1 0.3 copy.56
  103.4 13.0 %all_to_all.16 = bf16[16,8,384]{2,1,0:T(8,128)(2,1)S(1)} all-to-all(bf16[16,8,384]{2,1,0:T(8,128)(2,1)S(1)} %copy.56), channel_id=1, replica_groups=mesh['row'=8,'col'=16] {'col'}, dimensions={0} | all-to-all | bytes 196608 | tf_op jit(solution)/shard_map/all_to_all | solution.py:47
  116.4 1.8 reshape.109
  118.2 3.8 multiply_reduce_fusion.3
  122.1 29.9 %all-reduce.2 = (f32[8]{0:T(128)S(1)}, f32[8]{0:T(128)S(1)}) all-reduce(f32[8]{0:T(128)S(1)} %get-tuple-element.9, f32[8]{0:T(128)S(1)} %get-tuple-element.13), channel_id=1, replica_groups=mesh['row'=8,'col'=16] {'col'}, use_global_device_ids=true, to_apply=%region_2.0 | all-reduce | flops 16 | bytes 128 | tf_op jit(solution)/shard_map/psum | solution.py:38
  152.0 23.4 %psum.59 = f32[8]{0:T(128)S(1)} all-reduce(f32[8]{0:T(128)S(1)} %get-tuple-element.6), channel_id=1, replica_groups=mesh['row'=8,'col'=16] {'row'}, use_global_device_ids=true, to_apply=%region_5.0 | all-reduce | flops 8 | bytes 64 | tf_op jit(solution)/shard_map/psum | solution.py:54
  175.5 9.4 %fusion.31 = bf16[1,128,384]{1,2,0:T(8,128)(2,1)S(1)} fusion(bf16[128,48,512]{2,1,0:T(8,128)(2,1)} %bitcast.81, f32[8,512]{1,0:T(8,128)S(1)} %copy-done.4, f32[8,512]{1,0:T(8,128)S(1)} %get-tuple-element.14, f32[8]{0:T(128)S(1)} %add_divide_fusion.1), kind=kOutput, calls=%fused_computation.18 | convolution fusion | flops 50393088 | bytes 6422560 | tf_op jit(solution)/shard_map/ijsp,dip->ijsd/dot_general | solution.py:25
  184.9 0.2 copy.59
  185.1 1.2 reduce.7
  186.3 9.2 %all_to_all.17 = bf16[16,2,1536]{2,1,0:T(2,128)(2,1)S(1)} all-to-all(bf16[16,2,1536]{2,1,0:T(2,128)(2,1)S(1)} %reshape.131), channel_id=1, replica_groups=mesh['row'=8,'col'=16] {'col'}, dimensions={0} | all-to-all | bytes 196608 | tf_op jit(solution)/shard_map/all_to_all | solution.py:31
  195.7 0.6 bitcast_reduce_fusion
  196.2 1.8 reshape.111
  198.0 4.8 fusion.6
  202.8 54.5 %all-reduce.9.cloned.1.call-done = f32[8,4096]{1,0:T(8,128)} async-done(((f32[8,4096]{1,0:T(8,128)}), f32[8,4096]{1,0:T(8,128)}) %all-reduce.9.cloned.1.call-update) | async-done | bytes 131088 | tf_op jit(solution)/shard_map/psum | solution.py:36
  257.3 1.1 fusion.51
  258.4 5.9 %fusion.25 = bf16[16,8,48,8]{2,3,0,1:T(8,128)(2,1)S(1)} fusion(bf16[8,8,512,1]{2,0,3,1:T(8,128)(2,1)S(1)} %bitcast.90, bf16[16,8,48,512]{3,2,1,0:T(8,128)(2,1)} %param.9, f32[16,8,48]{2,0,1:T(8,128)S(1)} %get-tuple-element.11), kind=kOutput, calls=%fused_computation.16 | convolution fusion | flops 50429952 | bytes 6479872 | tf_op jit(solution)/shard_map/ijsp,djp->ijsd/dot_general | solution.py:41
  264.2 0.5 copy.62
  264.8 0.9 copy.63
  265.7 6.5 %all-to-all-start.3 = ((bf16[16,8,384]{2,1,0:T(8,128)(2,1)}), bf16[16,8,384]{2,1,0:T(8,128)(2,1)S(1)}, u32[]{:S(2)}, u32[]{:S(2)}) async-start(bf16[16,8,384]{2,1,0:T(8,128)(2,1)} %copy.63), calls=%async_computation.3 | async-start | bytes 196608 | tf_op jit(solution)/shard_map/all_to_all | solution.py:47
  272.3 0.2 dynamic-slice_reduce_fusion
  272.5 6.4 %all-to-all-done.3 = bf16[16,8,384]{2,1,0:T(8,128)(2,1)S(1)} async-done(((bf16[16,8,384]{2,1,0:T(8,128)(2,1)}), bf16[16,8,384]{2,1,0:T(8,128)(2,1)S(1)}, u32[]{:S(2)}, u32[]{:S(2)}) %all-to-all-start.3) | async-done | bytes 98336 | tf_op jit(solution)/shard_map/all_to_all | solution.py:47
  278.9 1.8 reshape.115
  280.7 3.8 multiply_reduce_fusion.2
  284.6 29.9 %all-reduce.1 = (f32[8]{0:T(128)S(1)}, f32[8]{0:T(128)S(1)}) all-reduce(f32[8]{0:T(128)S(1)} %get-tuple-element.8, f32[8]{0:T(128)S(1)} %get-tuple-element.15), channel_id=1, replica_groups=mesh['row'=8,'col'=16] {'col'}, use_global_device_ids=true, to_apply=%region_8.0 | all-reduce | flops 16 | bytes 128 | tf_op jit(solution)/shard_map/psum | solution.py:38
  314.5 23.3 %psum.63 = f32[8]{0:T(128)S(1)} all-reduce(f32[8]{0:T(128)S(1)} %get-tuple-element.4), channel_id=1, replica_groups=mesh['row'=8,'col'=16] {'row'}, use_global_device_ids=true, to_apply=%region_11.0 | all-reduce | flops 8 | bytes 64 | tf_op jit(solution)/shard_map/psum | solution.py:54
  337.8 0.1 multiply_add_fusion
  337.9 5.7 %convolution_bitcast_fusion = f32[1,2,8,512]{3,2,1,0:T(8,128)S(1)} fusion(bf16[2,512,4096]{2,1,0:T(8,128)(2,1)} %param.11, f32[8,4096]{1,0:T(8,128)S(1)} %multiply_add_fusion), kind=kOutput, calls=%fused_computation.19 | convolution fusion | flops 67141632 | bytes 8552448 | tf_op jit(solution)/shard_map/bpn,dn->bdp/dot_general | solution.py:60
  343.6 2.4 fusion.44
  346.1 0.7 multiply_subtract_fusion
  346.7 144.0 %all-reduce.11.cloned.1.call-done = f32[128,4096]{1,0:T(8,128)} async-done(((f32[128,4096]{1,0:T(8,128)}), f32[128,4096]{1,0:T(8,128)}) %all-reduce.11.cloned.1.call-update) | async-done | bytes 2097168
  490.7 1.5 constant_dynamic-slice_fusion
  (26 shorter events, 0.4 us)
Async XLA Ops:
  7.2 265.1 %copy-start = (s32[16,16]{1,0:T(8,128)S(1)}, s32[16,16]{1,0:T(8,128)}, u32[]{:S(2)}) copy-start(s32[16,16]{1,0:T(8,128)} %param.12) | copy-start | bytes 3076
  7.2 16.4 %copy-start.5 = (s32[16,8]{0,1:T(8,128)S(1)}, s32[16,8]{0,1:T(8,128)}, u32[]{:S(2)}) copy-start(s32[16,8]{0,1:T(8,128)} %param.10) | copy-start | bytes 1540
  15.9 14.3 %all-to-all-start = ((bf16[16,2,1536]{2,1,0:T(2,128)(2,1)}), bf16[16,2,1536]{2,1,0:T(2,128)(2,1)S(1)}, u32[]{:S(2)}, u32[]{:S(2)}) async-start(bf16[16,2,1536]{2,1,0:T(2,128)(2,1)} %reshape.129), calls=%async_computation | async-start | bytes 196608 | tf_op jit(solution)/shard_map/all_to_all | solution.py:31
  23.5 72.1 %all-reduce.7.cloned.1.call-start = ((), (), s32[]{:S(2)}) async-start(), calls=%async_computation.4 | async-start | bytes 262144 | tf_op jit(solution)/shard_map/psum | solution.py:36
  37.4 219.8 %all-reduce.9.cloned.1.call-start = ((), (), s32[]{:S(2)}) async-start(), calls=%async_computation.5 | async-start | bytes 262144 | tf_op jit(solution)/shard_map/psum | solution.py:36
  102.6 72.9 %copy-start.4 = (f32[8,512]{1,0:T(8,128)S(1)}, f32[8,512]{1,0:T(8,128)}, u32[]{:S(2)}) copy-start(f32[8,512]{1,0:T(8,128)} %param.7) | copy-start | bytes 49156
  264.2 73.5 %copy-start.2 = (f32[8,4096]{1,0:T(8,128)S(1)}, f32[8,4096]{1,0:T(8,128)}, u32[]{:S(2)}) copy-start(f32[8,4096]{1,0:T(8,128)} %all-reduce.7.cloned.1.call-done) | copy-start | bytes 393220
  264.2 73.5 %copy-start.3 = (f32[8,4096]{1,0:T(8,128)S(1)}, f32[8,4096]{1,0:T(8,128)}, u32[]{:S(2)}) copy-start(f32[8,4096]{1,0:T(8,128)} %all-reduce.9.cloned.1.call-done) | copy-start | bytes 393220
  265.7 13.2 %all-to-all-start.3 = ((bf16[16,8,384]{2,1,0:T(8,128)(2,1)}), bf16[16,8,384]{2,1,0:T(8,128)(2,1)S(1)}, u32[]{:S(2)}, u32[]{:S(2)}) async-start(bf16[16,8,384]{2,1,0:T(8,128)(2,1)} %copy.63), calls=%async_computation.3 | async-start | bytes 196608 | tf_op jit(solution)/shard_map/all_to_all | solution.py:47
  272.2 218.5 %all-reduce.11.cloned.1.call-start = ((), (), s32[]{:S(2)}) async-start(), calls=%async_computation.6 | async-start | bytes 4194304
  284.6 59.1 %copy-start.6 = (s32[128]{0:T(128)S(1)}, s32[128]{0:T(128)}, u32[]{:S(2)}) copy-start(s32[128]{0:T(128)} %param.13) | copy-start | bytes 1540
  337.9 8.2 %copy-start.1 = (f32[8,4096]{1,0:T(8,128)}, f32[8,4096]{1,0:T(8,128)S(1)}, u32[]{:S(2)}) copy-start(f32[8,4096]{1,0:T(8,128)S(1)} %multiply_add_fusion) | copy-start | bytes 393220
Sparse Core Ops, SparseCore 0:
  37.6 58.0 all-reduce.6
  202.9 54.2 all-reduce.8
  346.2 144.5 all-reduce.10
